TPU v7x, 32 devices: a whole 2x2x4 slice. The times are simulated.
32 devices in a mesh: wide: 16 (over z, y, x), narrow: 2 (over core).
Axes of the slice: x: 2, y: 2, z: 4, core: 2. Of those that a mesh axis runs over, the one named last changes fastest.
Arguments:
- queries: bfloat16 [4096, 768], P(('wide', 'narrow')), may hold values from -40 to 40
- table: bfloat16 [2048, 768], P('wide'), may hold values from -6 to 6
- head: bfloat16 [768, 768], replicated, may hold values from -0.21875 to 0.21875
- pos_ids: int32 [4096], P(('wide', 'narrow')), may hold values from 0 to 2047, as said below
- neg_ids: int32 [4096, 8], P(('wide', 'narrow')), may hold values from 0 to 2047, as said below
- loss_weights: float32 [4096], P(('wide', 'narrow')), may hold values from 8 to 64
Outputs:
- d_queries: float32 [4096, 768], P(('wide', 'narrow'))
- d_table: float32 [2048, 768], P(('wide', 'narrow'))
- d_head: float32 [768, 768], replicated
Inputs may be any that keep to these rules, and one draw needn't show every extreme that they name: `pos_ids`: the queries form aligned blocks of 128 (the queries of one device). Within a block at most 16 positives lie in one shard of 128 consecutive passage rows (shard = id // 128); one shard, the same for every block, holds exactly 16 of every block. `neg_ids`: within each aligned block of 128 queries, at most 96 of its 1024 negatives lie in one shard of 128 consecutive passage rows (shard = id // 128); one shard, the same for every block, holds exactly 96 of every block. Popular rows recur.
All inputs are finite; a program needn't handle non-finite values.
Results may differ from a plain program's by a relative error of at most 0.0063.
Values may be sent and summed in bfloat16 or wider, within the bound.
A program may use at most 64 MiB of HBM per device.

v0:
```python
import jax
import jax.numpy as jnp
from jax import lax
from jax.sharding import PartitionSpec as P


def slot_places(flat_ids, shard_rows, wide_count, capacity):
    owner_shard = flat_ids // shard_rows
    local_rows = flat_ids % shard_rows
    membership = (owner_shard[:, None] == jnp.arange(wide_count, dtype=jnp.int32)[None, :]).astype(
        jnp.int32
    )
    ranked = jnp.sum(jnp.cumsum(membership, axis=0) * membership, axis=1) - 1
    target = owner_shard * capacity + ranked
    requests = jnp.zeros((wide_count * capacity,), jnp.int32).at[target].set(local_rows)
    return (requests.reshape(wide_count, capacity), target)


def per_device(queries, table, head, pos_ids, neg_ids, loss_weights):
    wide_count = lax.axis_size("wide")
    narrow_count = lax.axis_size("narrow")
    batch_rows = queries.shape[0]
    width = queries.shape[1]
    shard_rows = table.shape[0]
    negatives = neg_ids.shape[1]
    pos_capacity = max(2, 2 * batch_rows // wide_count)
    neg_capacity = max(2, 3 * negatives * batch_rows // (2 * wide_count))
    scale = float(width) ** (-0.5)
    mine = lax.axis_index("narrow")
    pos_requests, pos_target = slot_places(pos_ids, shard_rows, wide_count, pos_capacity)
    neg_requests, neg_target = slot_places(
        neg_ids.reshape(-1), shard_rows, wide_count, neg_capacity
    )
    requests = jnp.concatenate([pos_requests, neg_requests], axis=1)
    received = lax.all_to_all(requests, "wide", split_axis=0, concat_axis=0, tiled=True)
    picked = jnp.take(table, received, axis=0)
    fetched = lax.all_to_all(picked, "wide", split_axis=0, concat_axis=0, tiled=True)
    pos_rows = fetched[:, :pos_capacity].reshape(-1, width)[pos_target]
    neg_rows = fetched[:, pos_capacity:].reshape(-1, width)[neg_target]
    query_proj = jnp.dot(queries, head, preferred_element_type=jnp.float32).astype(jnp.bfloat16)
    key_proj = jnp.dot(pos_rows, head, preferred_element_type=jnp.float32).astype(jnp.bfloat16)
    neg_proj = jnp.dot(neg_rows, head, preferred_element_type=jnp.float32).astype(jnp.bfloat16)
    neg_proj = neg_proj.reshape(batch_rows, negatives, width)
    keys_all = lax.all_gather(key_proj, "narrow", axis=0, tiled=True)
    group = keys_all.shape[0]
    in_scores = (
        lax.dot_general(
            query_proj, keys_all, (((1,), (1,)), ((), ())), preferred_element_type=jnp.float32
        )
        * scale
    )
    neg_scores = (
        jnp.einsum("bd,bnd->bn", query_proj, neg_proj, preferred_element_type=jnp.float32) * scale
    )
    top = jnp.maximum(jnp.max(in_scores, axis=1), jnp.max(neg_scores, axis=1))
    total = jnp.sum(jnp.exp(in_scores - top[:, None]), axis=1) + jnp.sum(
        jnp.exp(neg_scores - top[:, None]), axis=1
    )
    log_total = top + jnp.log(total)
    in_probs = jnp.exp(in_scores - log_total[:, None])
    neg_probs = jnp.exp(neg_scores - log_total[:, None])
    own_column = mine * batch_rows + jnp.arange(batch_rows, dtype=jnp.int32)
    columns = jnp.arange(group, dtype=jnp.int32)
    target_mark = (columns[None, :] == own_column[:, None]).astype(jnp.float32)
    in_coef = (loss_weights[:, None] * (in_probs - target_mark) * scale).astype(jnp.bfloat16)
    neg_coef = (loss_weights[:, None] * neg_probs * scale).astype(jnp.bfloat16)
    grad_query = jnp.dot(in_coef, keys_all, preferred_element_type=jnp.float32)
    grad_query = grad_query + jnp.einsum(
        "bn,bnd->bd", neg_coef, neg_proj, preferred_element_type=jnp.float32
    )
    grad_query = grad_query.astype(jnp.bfloat16)
    d_queries = lax.dot_general(
        grad_query, head, (((1,), (1,)), ((), ())), preferred_element_type=jnp.float32
    )
    key_grad = lax.psum_scatter(
        lax.dot_general(
            in_coef, query_proj, (((0,), (0,)), ((), ())), preferred_element_type=jnp.float32
        ),
        "narrow",
        scatter_dimension=0,
        tiled=True,
    )
    pos_buffer = (
        jnp.zeros((wide_count * pos_capacity, width), jnp.float32).at[pos_target].set(key_grad)
    )
    pos_buffer = pos_buffer.reshape(wide_count, pos_capacity, width)
    pos_back = lax.all_to_all(pos_buffer, "wide", split_axis=0, concat_axis=0, tiled=True)
    repeated = jnp.repeat(query_proj, negatives, axis=0)
    neg_vectors = (
        jnp.zeros((wide_count * neg_capacity, width), jnp.bfloat16).at[neg_target].set(repeated)
    )
    neg_vectors = neg_vectors.reshape(wide_count, neg_capacity, width)
    neg_weights = (
        jnp.zeros((wide_count * neg_capacity,), jnp.bfloat16)
        .at[neg_target]
        .set(neg_coef.reshape(-1))
    )
    neg_weights = neg_weights.reshape(wide_count, neg_capacity)
    vectors_back, weights_back = (
        lax.all_to_all(neg_vectors, "wide", split_axis=0, concat_axis=0, tiled=True),
        lax.all_to_all(neg_weights, "wide", split_axis=0, concat_axis=0, tiled=True),
    )
    neg_back = vectors_back.astype(jnp.float32) * weights_back.astype(jnp.float32)[:, :, None]
    returned = jnp.concatenate([pos_back, neg_back], axis=1)
    row_partial = jax.ops.segment_sum(
        returned.reshape(-1, width), received.reshape(-1), num_segments=shard_rows
    )
    row_total = lax.psum_scatter(row_partial, "narrow", scatter_dimension=0, tiled=True)
    row_grad = row_total.astype(jnp.bfloat16)
    d_table = lax.dot_general(
        row_grad, head, (((1,), (1,)), ((), ())), preferred_element_type=jnp.float32
    )
    part_rows = shard_rows // narrow_count
    my_table = lax.dynamic_slice_in_dim(table, mine * part_rows, part_rows, 0)
    head_part = lax.dot_general(
        queries, grad_query, (((0,), (0,)), ((), ())), preferred_element_type=jnp.float32
    )
    head_part = head_part + lax.dot_general(
        my_table, row_grad, (((0,), (0,)), ((), ())), preferred_element_type=jnp.float32
    )
    d_head = lax.psum(head_part, ("wide", "narrow"))
    return (d_queries, d_table, d_head)


def solution(mesh):
    placed = (
        P(("wide", "narrow"), None),
        P("wide", None),
        P(),
        P(("wide", "narrow")),
        P(("wide", "narrow"), None),
        P(("wide", "narrow")),
    )
    return jax.shard_map(
        per_device,
        mesh=mesh,
        in_specs=placed,
        out_specs=(P(("wide", "narrow"), None), P(("wide", "narrow"), None), P()),
        check_vma=False,
    )
```

profile of v0, /device:TPU:0, one launch (start us, length us, event | category | flops | bytes accessed | tf_op | source)
XLA Modules:
  0.0 382.6 jit_solution(5747865731320632928)
XLA Ops:
  8.4 4.5 %reduce-window.6 = s32[16,8,128]{2,1,0:T(8,128)S(1)} reduce-window(s32[16,8,128]{2,1,0:T(8,128)S(1)} %fusion.19, s32[]{:T(128)} %constant.84.clone.1), window={size=1x1x128 pad=0_0x0_0x127_0}, to_apply=%region_3.4 | reduce-window | flops 2080768 | bytes 131076 | tf_op jit(solution)/shard_map/reduce-window
  13.4 4.3 %scatter_custom_fusion.1 = s32[1536]{0:T(1024)S(1)} fusion(s32[1024]{0:T(1024)S(1)} %bitcast.76, s32[1024]{0:T(1024)S(1)} %get-tuple-element.15, s32[]{:T(128)} %constant.84.clone.1), kind=kCustom, calls=%fused_computation.76 | custom fusion | bytes 6148 | tf_op jit(solution)/shard_map/scatter | solution.py:15
  20.1 15.4 %all_to_all.40 = s32[16,1,112]{2,1,0:T(1,128)S(1)} all-to-all(s32[16,1,112]{2,1,0:T(1,128)S(1)} %bitcast.73), channel_id=1, replica_groups=mesh['wide'=16,'narrow'=2] {'wide'}, dimensions={0} | all-to-all | bytes 14336 | tf_op jit(solution)/shard_map/all_to_all | solution.py:35
  35.7 6.4 %gather_fusion = bf16[1792,768]{1,0:T(8,128)(2,1)} fusion(bf16[128,768]{1,0:T(8,128)(2,1)S(1)} %copy-done.1, s32[2048]{0:T(1024)S(1)} %pad_clamp_fusion), kind=kCustom, calls=%fused_computation | custom fusion | bytes 5512192 | tf_op jit(solution)/shard_map/jit(_take)/gather | solution.py:36
  42.0 3.1 broadcast_select_fusion
  45.1 4.6 %all-to-all-start.1 = ((bf16[16,112,768]{2,1,0:T(8,128)(2,1)}), bf16[16,112,768]{2,1,0:T(8,128)(2,1)}, u32[]{:S(2)}, u32[]{:S(2)}) async-start(bf16[16,112,768]{2,1,0:T(8,128)(2,1)} %broadcast_select_fusion), calls=%async_computation.1 | async-start | bytes 5505024 | tf_op jit(solution)/shard_map/all_to_all | solution.py:37
  50.1 6.9 %scatter_custom_fusion.3 = bf16[1536,768]{1,0:T(8,128)(2,1)} fusion(s32[1024]{0:T(1024)S(1)} %bitcast.77, bf16[]{:T(256)} %constant.99.clone.1, bf16[128,768]{1,0:T(8,128)(2,1)S(1)} %convolution_convert_fusion.2), kind=kCustom, calls=%fused_computation.14 | custom fusion | bytes 2555906 | tf_op jit(solution)/shard_map/scatter | solution.py:90
  57.0 46.1 %all-to-all-done.1 = bf16[16,112,768]{2,1,0:T(8,128)(2,1)} async-done(((bf16[16,112,768]{2,1,0:T(8,128)(2,1)}), bf16[16,112,768]{2,1,0:T(8,128)(2,1)}, u32[]{:S(2)}, u32[]{:S(2)}) %all-to-all-start.1) | async-done | bytes 2752544 | tf_op jit(solution)/shard_map/all_to_all | solution.py:37
  103.1 12.5 %all-to-all-start.3 = ((bf16[16,96,768]{2,1,0:T(8,128)(2,1)}), bf16[16,96,768]{2,1,0:T(8,128)(2,1)}, u32[]{:S(2)}, u32[]{:S(2)}) async-start(bf16[16,96,768]{2,1,0:T(8,128)(2,1)} %bitcast.63), calls=%async_computation.4 | async-start | bytes 4718592 | tf_op jit(solution)/shard_map/all_to_all | solution.py:100
  117.3 1.5 gather_fusion.1
  118.8 3.2 slice.25
  122.0 6.5 %gather_fusion.2 = bf16[1024,768]{1,0:T(8,128)(2,1)S(1)} fusion(bf16[1536,768]{1,0:T(8,128)(2,1)} %bitcast.60, s32[1024]{0:T(1024)S(1)} %broadcast_clamp_fusion), kind=kCustom, calls=%fused_computation.2 | custom fusion | bytes 3149824 | tf_op jit(solution)/shard_map/gather | solution.py:39
  128.9 2.3 all_gather.3
  131.1 1.4 convolution_convert_fusion
  134.6 1.3 fusion.34
  136.1 7.6 %scatter_custom_fusion.4 = bf16[1536]{0:T(1024)(128)(2,1)S(1)} fusion(s32[1024]{0:T(1024)S(1)} %bitcast.79, bf16[1024]{0:T(1024)(128)(2,1)S(1)} %reshape.311, bf16[]{:T(256)} %constant.99.clone.1), kind=kCustom, calls=%fused_computation.83 | custom fusion | bytes 3074 | tf_op jit(solution)/shard_map/scatter | solution.py:96
  144.4 18.3 %all-to-all-done.3 = bf16[16,96,768]{2,1,0:T(8,128)(2,1)} async-done(((bf16[16,96,768]{2,1,0:T(8,128)(2,1)}), bf16[16,96,768]{2,1,0:T(8,128)(2,1)}, u32[]{:S(2)}, u32[]{:S(2)}) %all-to-all-start.3) | async-done | bytes 2359328 | tf_op jit(solution)/shard_map/all_to_all | solution.py:100
  162.7 10.9 %all-to-all-start.4 = ((bf16[16,1,96]{2,1,0:T(2,128)(2,1)}), bf16[16,1,96]{2,1,0:T(2,128)(2,1)S(1)}, u32[]{:S(2)}, u32[]{:S(2)}) async-start(bf16[16,1,96]{2,1,0:T(2,128)(2,1)} %all_to_all.34), calls=%async_computation.5 | async-start | bytes 16384 | tf_op jit(solution)/shard_map/all_to_all | solution.py:101
  173.6 2.4 scatter_custom_fusion.2
  176.0 4.8 %all-to-all-done.4 = bf16[16,1,96]{2,1,0:T(2,128)(2,1)S(1)} async-done(((bf16[16,1,96]{2,1,0:T(2,128)(2,1)}), bf16[16,1,96]{2,1,0:T(2,128)(2,1)S(1)}, u32[]{:S(2)}, u32[]{:S(2)}) %all-to-all-start.4) | async-done | bytes 3104 | tf_op jit(solution)/shard_map/all_to_all | solution.py:101
  180.8 3.6 all-to-all-start.2
  185.9 4.3 %convert_multiply_fusion = f32[16,96,768]{2,1,0:T(8,128)} fusion(bf16[16,96,768]{2,1,0:T(8,128)(2,1)} %all-to-all-done.3, f32[16,96]{1,0:T(8,128)S(1)} %bitcast.74), kind=kLoop, calls=%fused_computation.10 | loop fusion | flops 2359296 | bytes 7084032 | tf_op jit(solution)/shard_map/mul | solution.py:103
  190.2 12.6 %all-to-all-done.2 = f32[16,16,768]{2,1,0:T(8,128)S(1)} async-done(((f32[16,16,768]{2,1,0:T(8,128)}), f32[16,16,768]{2,1,0:T(8,128)S(1)}, u32[]{:S(2)}, u32[]{:S(2)}) %all-to-all-start.2) | async-done | bytes 786464 | tf_op jit(solution)/shard_map/all_to_all | solution.py:87
  202.8 5.2 %pad_maximum_fusion = f32[16,112,768]{2,1,0:T(8,128)} fusion(f32[16,96,768]{2,1,0:T(8,128)} %convert_multiply_fusion, f32[16,16,768]{2,1,0:T(8,128)S(1)} %all-to-all-done.2), kind=kLoop, calls=%fused_computation.9 | loop fusion | flops 1376256 | bytes 11010048 | tf_op jit(solution)/shard_map/concatenate | solution.py:104
  207.9 15.4 %scatter_custom_fusion.5 = f32[128,768]{1,0:T(8,128)} fusion(s32[1792]{0:T(1024)S(1)} %reshape.317, f32[1792,768]{1,0:T(8,128)} %bitcast.64, f32[]{:T(128)} %constant.97.clone.1), kind=kCustom, calls=%fused_computation.30 | custom fusion | flops 1376256 | bytes 393728 | tf_op jit(solution)/shard_map/scatter-add | solution.py:105
  223.4 2.0 fusion.2
  225.7 1.9 fusion.37
  227.6 2.6 reduce-scatter.5.cloned.1.call-done
  230.1 3.7 bitcast_add_fusion
  233.9 1.3 fusion.36
  236.3 136.7 %all-reduce.2.cloned.1.call-done = f32[768,768]{0,1:T(8,128)} async-done(((f32[768,768]{0,1:T(8,128)}), f32[768,768]{0,1:T(8,128)}) %all-reduce.2.cloned.1.call-update) | async-done | bytes 2359312 | tf_op jit(solution)/shard_map/psum | solution.py:121
  373.0 3.0 copy.34
  (79 shorter events, 12.2 us)
Async XLA Ops:
  7.2 42.6 %copy-start = (bf16[768,768]{1,0:T(8,128)(2,1)S(1)}, bf16[768,768]{1,0:T(8,128)(2,1)}, u32[]{:S(2)}) copy-start(bf16[768,768]{1,0:T(8,128)(2,1)} %param.8) | copy-start | bytes 3538948
  7.2 28.5 %copy-start.1 = (bf16[128,768]{1,0:T(8,128)(2,1)S(1)}, bf16[128,768]{1,0:T(8,128)(2,1)}, u32[]{:S(2)}) copy-start(bf16[128,768]{1,0:T(8,128)(2,1)} %param.7) | copy-start | bytes 589828
  18.9 97.3 %copy-start.9 = (s32[128]{0:T(128)}, s32[128]{0:T(128)S(1)}, u32[]{:S(2)}) copy-start(s32[128]{0:T(128)S(1)} %compare_select_fusion.6) | copy-start | bytes 1540
  45.1 4.6 %copy-start.4 = (bf16[128,768]{1,0:T(8,128)(2,1)S(1)}, bf16[128,768]{1,0:T(8,128)(2,1)}, u32[]{:S(2)}) copy-start(bf16[128,768]{1,0:T(8,128)(2,1)} %param.6) | copy-start | bytes 589828
  45.1 58.0 %all-to-all-start.1 = ((bf16[16,112,768]{2,1,0:T(8,128)(2,1)}), bf16[16,112,768]{2,1,0:T(8,128)(2,1)}, u32[]{:S(2)}, u32[]{:S(2)}) async-start(bf16[16,112,768]{2,1,0:T(8,128)(2,1)} %broadcast_select_fusion), calls=%async_computation.1 | async-start | bytes 5505024 | tf_op jit(solution)/shard_map/all_to_all | solution.py:37
  103.1 59.6 %all-to-all-start.3 = ((bf16[16,96,768]{2,1,0:T(8,128)(2,1)}), bf16[16,96,768]{2,1,0:T(8,128)(2,1)}, u32[]{:S(2)}, u32[]{:S(2)}) async-start(bf16[16,96,768]{2,1,0:T(8,128)(2,1)} %bitcast.63), calls=%async_computation.4 | async-start | bytes 4718592 | tf_op jit(solution)/shard_map/all_to_all | solution.py:100
  115.6 58.0 %reduce-scatter.3.cloned.1.call-start = ((), (), s32[]{:S(2)}) async-start(), calls=%async_computation.7 | async-start | bytes 1179648 | tf_op jit(solution)/shard_map/reduce_scatter | solution.py:75
  122.0 6.5 %copy-start.3 = (bf16[128,768]{1,0:T(8,128)(2,1)S(1)}, bf16[128,768]{1,0:T(8,128)(2,1)}, u32[]{:S(2)}) copy-start(bf16[128,768]{1,0:T(8,128)(2,1)} %gather_fusion.1) | copy-start | bytes 589828
  132.5 1.1 copy-start.2
  132.6 2.0 copy-start.7
  132.6 2.0 copy-start.8
  162.7 18.1 %all-to-all-start.4 = ((bf16[16,1,96]{2,1,0:T(2,128)(2,1)}), bf16[16,1,96]{2,1,0:T(2,128)(2,1)S(1)}, u32[]{:S(2)}, u32[]{:S(2)}) async-start(bf16[16,1,96]{2,1,0:T(2,128)(2,1)} %all_to_all.34), calls=%async_computation.5 | async-start | bytes 16384 | tf_op jit(solution)/shard_map/all_to_all | solution.py:101
  180.8 22.0 %all-to-all-start.2 = ((f32[16,16,768]{2,1,0:T(8,128)}), f32[16,16,768]{2,1,0:T(8,128)S(1)}, u32[]{:S(2)}, u32[]{:S(2)}) async-start(f32[16,16,768]{2,1,0:T(8,128)} %bitcast.16), calls=%async_computation.3 | async-start | bytes 1572864 | tf_op jit(solution)/shard_map/all_to_all | solution.py:87
  184.4 45.7 %reduce-scatter.5.cloned.1.call-start = ((), (), s32[]{:S(2)}) async-start(), calls=%async_computation.8 | async-start | bytes 589824 | tf_op jit(solution)/shard_map/reduce_scatter | solution.py:108
  207.9 17.7 %copy-start.5 = (bf16[128,768]{1,0:T(8,128)(2,1)S(1)}, bf16[128,768]{1,0:T(8,128)(2,1)}, u32[]{:S(2)}) copy-start(bf16[128,768]{1,0:T(8,128)(2,1)} %param.6) | copy-start | bytes 589828
  223.4 149.6 %all-reduce.2.cloned.1.call-start = ((), (), s32[]{:S(2)}) async-start(), calls=%async_computation.9 | async-start | bytes 4718592 | tf_op jit(solution)/shard_map/psum | solution.py:121
  233.8 1.3 copy-start.6
Sparse Core Ops, SparseCore 0:
  136.0 9.3 reduce-scatter.2
  223.5 6.5 reduce-scatter.4
  236.3 136.7 all-reduce.1
where the time goes:
time: 383 us
  waiting for transfers between devices  221 us (58%)
  local copies, waits for them, and re-layouts  47.2 us (12%)
  other arithmetic  35.8 us (9%)
  starting transfers between devices  31.7 us (8%)
  blocking collectives  17.7 us (5%)
  matrix products  14.8 us (4%)
  between operations  14.1 us (4%)
    psum x1, waiting for transfers between devices, per_device(): d_head = lax.psum(head_part, ('wide', 'narrow'))  137 us
    all_to_all x1, waiting for transfers between devices, per_device(): lax.all_to_all(picked, 'wide', split_axis=0, concat_axis=0, tiled=True)  46.1 us
    all_to_all x1, waiting for transfers between devices, per_device(): lax.all_to_all(neg_vectors, 'wide', split_axis=0, concat_axis=0, tiled=True)  18.3 us
    all_to_all x1, blocking collectives, per_device(): lax.all_to_all(requests, 'wide', split_axis=0, concat_axis=0, tiled=True)  15.4 us
    scatter-add x1, other arithmetic, per_device(): jax.ops.segment_sum(returned.reshape(-1, width), received.reshape(-1), nu...  15.4 us
    all_to_all x1, waiting for transfers between devices, per_device(): lax.all_to_all(pos_buffer, 'wide', split_axis=0, concat_axis=0, tiled=True)  12.6 us
    all_to_all x1, starting transfers between devices, per_device(): lax.all_to_all(neg_vectors, 'wide', split_axis=0, concat_axis=0, tiled=True)  12.5 us
    all_to_all x1, starting transfers between devices, per_device(): lax.all_to_all(neg_weights, 'wide', split_axis=0, concat_axis=0, tiled=True)  10.9 us
  transfers between devices with their start and end apart: 7, of which 6 were waited for; matrix products, arithmetic and copies ran while one was open for 12% of the time, Pallas kernels for 0%

commit v1 on v0

v1 whole, which is shorter than its diff:
```python
import jax
import jax.numpy as jnp
from jax import lax
from jax.sharding import PartitionSpec as P

BOTH = ("wide", "narrow")


def per_device(queries, table, head, pos_ids, neg_ids, loss_weights):
    wide_count = lax.axis_size("wide")
    narrow_count = lax.axis_size("narrow")
    width = queries.shape[1]
    shard_rows = table.shape[0]
    part_rows = shard_rows // narrow_count
    rows = shard_rows * wide_count
    scale = float(width) ** (-0.5)
    mine = lax.axis_index("narrow")
    my_table = lax.dynamic_slice_in_dim(table, mine * part_rows, part_rows, 0)
    my_proj = jnp.dot(my_table, head, preferred_element_type=jnp.float32).astype(jnp.bfloat16)
    table_proj = lax.all_gather(my_proj, BOTH, axis=0, tiled=True)
    group_pos = lax.all_gather(pos_ids, "narrow", axis=0, tiled=True)
    query_proj = jnp.dot(queries, head, preferred_element_type=jnp.float32).astype(jnp.bfloat16)
    columns = jnp.arange(rows, dtype=jnp.int32)
    key_count = jnp.sum((group_pos[:, None] == columns[None, :]).astype(jnp.float32), axis=0)
    own = (pos_ids[:, None] == columns[None, :]).astype(jnp.float32)
    count = jnp.broadcast_to(key_count[None, :], own.shape)
    for n in range(neg_ids.shape[1]):
        count = count + (neg_ids[:, n : n + 1] == columns[None, :]).astype(jnp.float32)
    scores = (
        lax.dot_general(
            query_proj, table_proj, (((1,), (1,)), ((), ())), preferred_element_type=jnp.float32
        )
        * scale
    )
    top = jnp.max(jnp.where(count > 0, scores, -jnp.inf), axis=1, keepdims=True)
    exps = jnp.where(count > 0, jnp.exp(jnp.minimum(scores - top, 0.0)), 0.0)
    total = jnp.sum(count * exps, axis=1, keepdims=True)
    probs = exps / total
    weight = loss_weights[:, None] * scale
    coef = (weight * probs).astype(jnp.bfloat16).astype(jnp.float32)
    own_coef = (weight * (probs - 1.0)).astype(jnp.bfloat16).astype(jnp.float32)
    coef = ((count - own) * coef + own * own_coef).astype(jnp.bfloat16)
    grad_query = jnp.dot(coef, table_proj, preferred_element_type=jnp.float32).astype(jnp.bfloat16)
    d_queries = lax.dot_general(
        grad_query, head, (((1,), (1,)), ((), ())), preferred_element_type=jnp.float32
    )
    row_partial = lax.dot_general(
        coef, query_proj, (((0,), (0,)), ((), ())), preferred_element_type=jnp.float32
    ).astype(jnp.bfloat16)
    pieces = lax.all_to_all(row_partial, BOTH, split_axis=0, concat_axis=0, tiled=True)
    row_grad = jnp.sum(pieces.reshape(-1, part_rows, width).astype(jnp.float32), axis=0)
    row_grad = row_grad.astype(jnp.bfloat16)
    d_table = lax.dot_general(
        row_grad, head, (((1,), (1,)), ((), ())), preferred_element_type=jnp.float32
    )
    head_part = lax.dot_general(
        queries, grad_query, (((0,), (0,)), ((), ())), preferred_element_type=jnp.float32
    )
    head_part = head_part + lax.dot_general(
        my_table, row_grad, (((0,), (0,)), ((), ())), preferred_element_type=jnp.float32
    )
    d_head = lax.psum(head_part, BOTH)
    return (d_queries, d_table, d_head)


def solution(mesh):
    placed = (
        P(BOTH, None),
        P("wide", None),
        P(),
        P(BOTH),
        P(BOTH, None),
        P(BOTH),
    )
    return jax.shard_map(
        per_device,
        mesh=mesh,
        in_specs=placed,
        out_specs=(P(BOTH, None), P(BOTH, None), P()),
        check_vma=False,
    )
```

time: 383 us -> 309 us (0.81)
  local copies, waits for them, and re-layouts: 47.2 us -> 6.83 us
  waiting for transfers between devices: 221 us -> 256 us
  other arithmetic: 35.8 us -> 5.46 us
  starting transfers between devices: 31.7 us -> 3.6 us
  blocking collectives: 17.7 us -> 2.09 us
  matrix products: 14.8 us -> 20.9 us
    all_gather x0 -> x1, waiting for transfers between devices: none -> 57.6 us  [per_device(): table_proj = lax.all_gather(my_proj, BOTH, axis=0, tiled=True)]
    all_to_all x4 -> x1, starting transfers between devices: 31.6 us -> 3.52 us  [per_device(): lax.all_to_all(row_partial, BOTH, split_axis=0, concat_axis=0, tiled=True)]
    scatter x5 -> x0, local copies, waits for them, and re-layouts: 22.1 us -> none  [the longest x1 7.59 us: per_device(): neg_weights = jnp.zeros((wide_count * neg_capacity,), jnp.bfloat16).at[ne...]
    all_to_all x4 -> x1, waiting for transfers between devices: 81.9 us -> 66.1 us  [per_device(): lax.all_to_all(row_partial, BOTH, split_axis=0, concat_axis=0, tiled=True)]
    all_to_all x1 -> x0, blocking collectives: 15.4 us -> none  [per_device(): lax.all_to_all(requests, 'wide', split_axis=0, concat_axis=0, tiled=True)]
    scatter-add x1 -> x0, other arithmetic: 15.4 us -> none  [per_device(): jax.ops.segment_sum(returned.reshape(-1, width), received.reshape(-1), nu...]
    gather x3 -> x0, local copies, waits for them, and re-layouts: 14.4 us -> none  [the longest x1 6.48 us: per_device(): neg_rows = fetched[:, pos_capacity:].reshape(-1, width)[neg_target]]
    dot_general x7 -> x4, matrix products: 6.44 us -> 13.9 us  [the longest x1 4.24 us: per_device(): lax.dot_general(coef, query_proj, (((0,), (0,)), ((), ())), preferred_ele...]
  transfers between devices with their start and end apart: 7 -> 3, of which waited for: 6 -> 3; matrix products, arithmetic and copies ran while one was open for 12% -> 3% of each run, Pallas kernels for 0% -> 0%
where the time goes in v1:
time: 309 us
  waiting for transfers between devices  256 us (83%)
  matrix products  20.9 us (7%)
  between operations  14.1 us (5%)
  local copies, waits for them, and re-layouts  6.83 us (2%)
  other arithmetic  5.46 us (2%)
  starting transfers between devices  3.6 us (1%)
    psum x1, waiting for transfers between devices, per_device(): d_head = lax.psum(head_part, BOTH)  132 us
    all_to_all x1, waiting for transfers between devices, per_device(): lax.all_to_all(row_partial, BOTH, split_axis=0, concat_axis=0, tiled=True)  66.1 us
    all_gather x1, waiting for transfers between devices, per_device(): table_proj = lax.all_gather(my_proj, BOTH, axis=0, tiled=True)  57.6 us
  transfers between devices with their start and end apart: 3, of which 3 were waited for; matrix products, arithmetic and copies ran while one was open for 3% of the time, Pallas kernels for 0%

profile of v1, /device:TPU:0, one launch (start us, length us, event | category | flops | bytes accessed | tf_op | source)
XLA Modules:
  0.0 308.6 jit_solution(17481606412836012648)
XLA Ops:
  7.2 0.0 copy-start
  7.2 0.0 all-gather.3.cloned.1.call-start
  7.2 1.2 copy-done
  8.4 1.9 convolution_convert_fusion.3
  10.3 0.0 all-gather.3.cloned.1.call-update
  10.3 2.1 all-gather
  12.4 0.3 convert_reduce_fusion
  12.8 0.7 broadcast_multiply_fusion
  13.4 1.0 slice_bitcast_fusion.7
  14.4 1.2 convolution_convert_fusion.2
  15.7 57.6 %all-gather.3.cloned.1.call-done = bf16[2048,768]{1,0:T(8,128)(2,1)} async-done(((bf16[64,768]{1,0:T(8,128)(2,1)}), bf16[2048,768]{1,0:T(8,128)(2,1)}) %all-gather.3.cloned.1.call-update) | async-done | bytes 3145744 | tf_op jit(solution)/shard_map/all_gather | solution.py:20
  73.3 3.7 %select_reduce_fusion = (f32[128]{0:T(128)S(1)}, f32[128,2048]{1,0:T(8,128)S(1)}) fusion(s32[128]{0:T(128)S(1)} %get-tuple-element.18, s32[128]{0:T(128)S(1)} %get-tuple-element.19, s32[128]{0:T(128)S(1)} %get-tuple-element.13, s32[128]{0:T(128)S(1)} %get-tuple-element.14, s32[128]{0:T(128)S(1)} %get-tuple-element.15, s32[128]{0:T(128)S(1)} %get-tuple-element.16, ...), kind=kOutput, calls=%fused_computation.13 | convolution fusion | flops 409993088 | bytes 4403712 | tf_op jit(solution)/shard_map/dot_general | solution.py:30
  77.0 1.5 multiply_reduce_fusion
  78.5 0.0 copy-done.5
  78.5 4.2 %convolution_convert_fusion = bf16[2048,768]{1,0:T(8,128)(2,1)} fusion(bf16[128,768]{1,0:T(8,128)(2,1)S(1)} %convolution_convert_fusion.2, f32[128,2048]{1,0:T(8,128)S(1)} %get-tuple-element.21, f32[128]{0:T(128)S(1)} %multiply_reduce_fusion, f32[128]{0:T(128)S(1)} %get-tuple-element.20, f32[128]{0:T(128)S(1)} %broadcast_multiply_fusion, ...), kind=kOutput, calls=%fused_computation | convolution fusion | flops 415498240 | bytes 4405248 | tf_op jit(solution)/shard_map/dot_general | solution.py:47
  82.8 3.5 %all-to-all-start = ((bf16[32,64,768]{2,1,0:T(8,128)(2,1)}), bf16[32,64,768]{2,1,0:T(8,128)(2,1)}, u32[]{:S(2)}, u32[]{:S(2)}) async-start(bf16[32,64,768]{2,1,0:T(8,128)(2,1)} %bitcast.35), calls=%async_computation | async-start | bytes 6291456 | tf_op jit(solution)/shard_map/all_to_all | solution.py:50
  86.3 0.0 all-reduce.2.cloned.1.call-start
  86.3 0.0 copy-start.2
  86.3 4.1 %convolution_convert_fusion.1 = bf16[128,768]{1,0:T(8,128)(2,1)S(1)} fusion(bf16[2048,768]{1,0:T(8,128)(2,1)} %all-gather.3.cloned.1.call-done, f32[128,2048]{1,0:T(8,128)S(1)} %get-tuple-element.21, f32[128]{0:T(128)S(1)} %multiply_reduce_fusion, f32[128]{0:T(128)S(1)} %get-tuple-element.20, f32[128]{0:T(128)S(1)} %broadcast_multiply_fusion, ...), kind=kOutput, calls=%fused_computation.5 | convolution fusion | flops 414023680 | bytes 4405248 | tf_op jit(solution)/shard_map/dot_general | solution.py:43
  90.4 0.0 copy-start.3
  90.4 0.7 copy-done.3
  91.1 0.0 copy-done.2
  91.1 0.5 fusion.7
  91.6 66.1 %all-to-all-done = bf16[32,64,768]{2,1,0:T(8,128)(2,1)} async-done(((bf16[32,64,768]{2,1,0:T(8,128)(2,1)}), bf16[32,64,768]{2,1,0:T(8,128)(2,1)}, u32[]{:S(2)}, u32[]{:S(2)}) %all-to-all-start) | async-done | bytes 3145760 | tf_op jit(solution)/shard_map/all_to_all | solution.py:50
  157.7 3.0 reduce_sum.32
  160.7 2.9 bitcast_add_fusion
  163.5 0.0 all-reduce.2.cloned.1.call-update
  163.5 0.9 copy-done.4
  164.4 1.3 fusion.5
  165.7 1.2 fusion.6
  166.9 131.8 %all-reduce.2.cloned.1.call-done = f32[768,768]{0,1:T(8,128)} async-done(((f32[768,768]{0,1:T(8,128)}), f32[768,768]{0,1:T(8,128)}) %all-reduce.2.cloned.1.call-update) | async-done | bytes 2359312 | tf_op jit(solution)/shard_map/psum | solution.py:62
  298.7 3.0 copy.14
  (4 shorter events, 0.0 us)
Async XLA Ops:
  7.2 1.3 copy-start
  7.2 66.1 %all-gather.3.cloned.1.call-start = ((), (), s32[]{:S(2)}) async-start(), calls=%async_computation.1 | async-start | bytes 3244032 | tf_op jit(solution)/shard_map/all_gather | solution.py:20
  73.3 5.2 %copy-start.5 = (s32[128]{0:T(128)S(1)}, s32[128]{0:T(128)}, u32[]{:S(2)}) copy-start(s32[128]{0:T(128)} %param.9) | copy-start | bytes 1540
  82.8 74.9 %all-to-all-start = ((bf16[32,64,768]{2,1,0:T(8,128)(2,1)}), bf16[32,64,768]{2,1,0:T(8,128)(2,1)}, u32[]{:S(2)}, u32[]{:S(2)}) async-start(bf16[32,64,768]{2,1,0:T(8,128)(2,1)} %bitcast.35), calls=%async_computation | async-start | bytes 6291456 | tf_op jit(solution)/shard_map/all_to_all | solution.py:50
  86.3 212.4 %all-reduce.2.cloned.1.call-start = ((), (), s32[]{:S(2)}) async-start(), calls=%async_computation.2 | async-start | bytes 4718592 | tf_op jit(solution)/shard_map/psum | solution.py:62
  86.3 4.8 %copy-start.2 = (bf16[128,768]{1,0:T(8,128)(2,1)S(1)}, bf16[128,768]{1,0:T(8,128)(2,1)}, u32[]{:S(2)}) copy-start(bf16[128,768]{1,0:T(8,128)(2,1)} %param.6) | copy-start | bytes 589828
  90.4 0.7 copy-start.3
  163.5 0.9 copy-start.4
  163.5 2.2 copy-start.1
Sparse Core Ops, SparseCore 0:
  11.4 61.7 all-gather.2
  163.7 135.0 all-reduce.1

commit v2 on v1

v2 whole, which is shorter than its diff:
```python
import functools

import jax
import jax.numpy as jnp
from jax import lax
from jax.experimental import pallas as pl
from jax.experimental.pallas import tpu as pltpu
from jax.sharding import PartitionSpec as P

BOTH = ("wide", "narrow")
MESH = pl.DeviceIdType.MESH
NT = (((1,), (1,)), ((), ()))
TN = (((0,), (0,)), ((), ()))
F32 = jnp.float32
BF16 = jnp.bfloat16


def dot(a, b, dims=(((1,), (0,)), ((), ()))):
    return lax.dot_general(a, b, dims, preferred_element_type=F32)


class Net:
    def __init__(self, wide, narrow, send_sem, recv_sem):
        self.wide, self.narrow, self.depth = wide, narrow, wide // 4
        self.send_sem, self.recv_sem = send_sem, recv_sem
        self.w = lax.axis_index("wide")
        self.n = lax.axis_index("narrow")
        self.z, self.y, self.x = self.w // 4, (self.w // 2) % 2, self.w % 2
        self.px = (self.w + 1 - 2 * self.x, self.n)
        self.py = (self.w + 2 - 4 * self.y, self.n)
        self.me = self.y * 2 + self.x
        self.xn = self.y * 2 + 1 - self.x
        self.yn = (1 - self.y) * 2 + self.x
        self.dg = (1 - self.y) * 2 + 1 - self.x
        self.base = self.n * 4
        self.used = 0
        self.started = []

    def zpeer(self, d):
        return (lax.rem(self.z + d, self.depth) * 4 + self.me, self.n)

    def zfrom(self, d):
        return lax.rem(self.z - d + self.depth, self.depth)

    def sibling(self, d):
        return (self.w, lax.rem(self.n + d, self.narrow))

    def sems(self, count):
        first = self.used
        self.used += count
        return first

    def send(self, src, dst, sem, device):
        copy = pltpu.make_async_remote_copy(
            src_ref=src,
            dst_ref=dst,
            send_sem=self.send_sem.at[sem],
            recv_sem=self.recv_sem.at[sem],
            device_id=device,
            device_id_type=MESH,
        )
        copy.start()
        self.started.append(copy)

    def arrive(self, dst, sem):
        pltpu.make_async_remote_copy(
            src_ref=dst,
            dst_ref=dst,
            send_sem=self.send_sem.at[sem],
            recv_sem=self.recv_sem.at[sem],
            device_id=self.px,
            device_id_type=MESH,
        ).wait_recv()

    def drain(self):
        for copy in self.started:
            copy.wait_send()
        self.started = []

    def barrier(self):
        sem = pltpu.get_barrier_semaphore()
        peers = [self.px, self.py]
        peers += [self.zpeer(d) for d in range(1, self.depth)]
        peers += [self.sibling(d) for d in range(1, self.narrow)]
        for peer in peers:
            pl.semaphore_signal(sem, inc=1, device_id=peer, device_id_type=MESH)
        pl.semaphore_wait(sem, len(peers))

    def gather(self, buf, during=None):
        depth, base, z = self.depth, self.base, self.z
        zs = self.sems(depth)
        xs, ys = self.sems(depth), self.sems(depth)
        ax, by = self.sems(depth), self.sems(depth)
        sib = self.sems(4 * self.narrow)

        def share(slot, block):
            for d in range(1, self.narrow):
                piece = buf.at[:, base + block]
                self.send(piece, piece, sib + slot * self.narrow + d, self.sibling(d))

        own = buf.at[:, base + self.me, z]
        for d in range(1, depth):
            self.send(own, own, zs + d, self.zpeer(d))
        self.send(own, own, xs, self.px)
        self.send(own, own, ys, self.py)
        if during is not None:
            during()
        for d in range(1, depth):
            piece = buf.at[:, base + self.me, self.zfrom(d)]
            self.arrive(piece, zs + d)
            self.send(piece, piece, xs + d, self.px)
            self.send(piece, piece, ys + d, self.py)
        share(0, self.me)
        for d in range(depth):
            k = self.zfrom(d) if d else z
            self.arrive(buf.at[:, base + self.yn, k], ys + d)
            piece = buf.at[0, base + self.yn, k]
            self.send(piece, piece, ax + d, self.px)
            self.arrive(buf.at[:, base + self.xn, k], xs + d)
            piece = buf.at[1, base + self.xn, k]
            self.send(piece, piece, by + d, self.py)
        share(1, self.yn)
        share(2, self.xn)
        for d in range(depth):
            k = self.zfrom(d) if d else z
            self.arrive(buf.at[0, base + self.dg, k], ax + d)
            self.arrive(buf.at[1, base + self.dg, k], by + d)
        share(3, self.dg)
        for d in range(1, self.narrow):
            theirs = lax.rem(self.n - d + self.narrow, self.narrow) * 4
            for slot, block in enumerate((self.me, self.yn, self.xn, self.dg)):
                self.arrive(buf.at[:, theirs + block], sib + slot * self.narrow + d)

    def start_scatter(self, out, r0):
        sib = self.sems(self.narrow)

        def give(d):
            theirs = lax.rem(self.n + d, self.narrow) * 4
            self.send(out.at[:, pl.ds(theirs, 4)], r0.at[d - 1], sib + d, self.sibling(d))

        return sib, give

    def scatter(self, sib, own, out, r0, r1, r2, stage, r3, during=None):
        base, depth = self.base, self.depth
        one, two, zs = self.sems(4), self.sems(2), self.sems(depth)
        for d in range(1, self.narrow):
            self.arrive(r0.at[d - 1], sib + d)

        def pair(h, block):
            total = own(h, block)
            for d in range(1, self.narrow):
                total = total + r0[d - 1, h, block].astype(F32)
            return total

        for slot, blocks in enumerate(((self.dg, self.dg), (self.xn, self.yn))):
            for h, peer in ((0, self.px), (1, self.py)):
                at = out.at[h, base + blocks[h]]
                at[...] = pair(h, blocks[h]).astype(BF16)
                self.send(at, r1.at[h, slot], one + 2 * slot + h, peer)
        for h, block, peer in ((0, self.yn, self.py), (1, self.xn, self.px)):
            self.arrive(r1.at[h, 0], one + h)
            at = out.at[h, base + block]
            total = pair(h, block) + r1[h, 0].astype(F32)
            if h == 0:
                stage[0] = total.astype(BF16)
                self.send(stage.at[0], r2.at[0], two, peer)
            else:
                stage[1] = total.astype(BF16)
                self.send(stage.at[1], r2.at[1], two + 1, peer)
        if during is not None:
            during()
        kept = []
        for h in range(2):
            self.arrive(r1.at[h, 1], one + 2 + h)
            self.arrive(r2.at[h], two + h)
            total = pair(h, self.me) + r1[h, 1].astype(F32) + r2[h].astype(F32)
            stage[2 + h] = total.astype(BF16)
        for d in range(1, depth):
            to = lax.rem(self.z + d, depth)
            self.send(stage.at[pl.ds(2, 2), to], r3.at[d - 1], zs + d, self.zpeer(d))
        z = self.z
        for h in range(2):
            total = own(h, self.me, z) + r1[h, 1, z].astype(F32) + r2[h, z].astype(F32)
            for d in range(1, self.narrow):
                total = total + r0[d - 1, h, self.me, z].astype(F32)
            kept.append(total)
        for d in range(1, depth):
            self.arrive(r3.at[d - 1], zs + d)
            for h in range(2):
                kept[h] = kept[h] + r3[d - 1, h].astype(F32)
        return kept


def kernel(
    wide, narrow, reduce_head,
    queries, table, head, ids, weights,
    d_queries, d_table, d_head,
    send_sem, recv_sem,
    tab, neg_count, key_count, scores, coef, qp_ref, gq_ref,
    own_grad, out_grad, r0, r1, r2, stage, r3,
    head_grad, *head_bufs,
):
    net = Net(wide, narrow, send_sem, recv_sem)
    width = queries.shape[1]
    half = width // 2
    part = tab.shape[3]
    batch = queries.shape[0]
    span = net.depth * part
    blocks = 4 * narrow
    negatives = ids.shape[1] - 1
    scale = float(width) ** (-0.5)
    halves = (slice(0, half), slice(half, width))
    base, me, z = net.base, net.me, net.z

    net.barrier()
    my_table = table[pl.ds(pl.multiple_of(net.n * part, part), part), :]
    my_proj = dot(my_table, head[...]).astype(BF16)
    for h in range(2):
        tab[h, base + me, z] = my_proj[:, halves[h]]

    def each_block(body, carry=None, count=blocks):
        if count <= 8:
            for b in range(count):
                carry = body(b, carry)
            return carry
        return lax.fori_loop(0, count, body, carry)

    def cols(b):
        return pl.ds(pl.multiple_of(b * span, span), span)

    def own_mask(b):
        column = b * span + lax.broadcasted_iota(jnp.int32, (batch, span), 1)
        return column, (ids[:, negatives : negatives + 1] == column).astype(F32)

    keys = net.sems(narrow)

    def prepare():
        def count(b, _):
            column, own = own_mask(b)
            key_count[0, :, cols(b)] = jnp.sum(own, axis=0, keepdims=True)
            total = jnp.zeros((batch, span), F32)
            for k in range(negatives):
                total = total + (ids[:, k : k + 1] == column).astype(F32)
            neg_count[:, cols(b)] = total
            return 0

        each_block(count, 0)
        for d in range(1, narrow):
            net.send(key_count.at[0], key_count.at[d], keys + d, net.sibling(d))
        qp_ref[...] = dot(queries[...], head[...]).astype(BF16)

    net.gather(tab, prepare)
    for d in range(1, narrow):
        net.arrive(key_count.at[d], keys + d)

    def tab_block(h, b):
        return tab[h, b].reshape(span, half)

    def score(b, top):
        total = key_count[0, :, cols(b)]
        for d in range(1, narrow):
            total = total + key_count[d, :, cols(b)]
        count = neg_count[:, cols(b)] + total
        neg_count[:, cols(b)] = count
        value = dot(qp_ref[:, halves[0]], tab_block(0, b), NT)
        value = (value + dot(qp_ref[:, halves[1]], tab_block(1, b), NT)) * scale
        value = jnp.where(count > 0, value, -jnp.inf)
        scores[:, cols(b)] = value
        return jnp.maximum(top, jnp.max(value, axis=1, keepdims=True))

    top = each_block(score, jnp.full((batch, 1), -jnp.inf, F32))

    def expo(b, total):
        value = jnp.exp(scores[:, cols(b)] - top)
        scores[:, cols(b)] = value
        return total + jnp.sum(neg_count[:, cols(b)] * value, axis=1, keepdims=True)

    total = each_block(expo, jnp.zeros((batch, 1), F32))
    inverse = 1.0 / total
    weight = weights[...] * scale

    def coefs(b, _):
        _, own = own_mask(b)
        prob = scores[:, cols(b)] * inverse
        plain = (weight * prob).astype(BF16).astype(F32)
        target = (weight * (prob - 1.0)).astype(BF16).astype(F32)
        value = (neg_count[:, cols(b)] - own) * plain + own * target
        coef[b] = value.astype(BF16)
        return 0

    each_block(coefs, 0)

    sib, give = net.start_scatter(out_grad, r0)
    for d in range(1, narrow):
        theirs = lax.rem(net.n + d, narrow) * 4
        for k in range(4):
            for h in range(2):
                grad = dot(coef[theirs + k], qp_ref[:, halves[h]], TN)
                out_grad[h, theirs + k] = grad.astype(BF16).reshape(net.depth, part, half)
        give(d)
    for k in range(4):
        for h in range(2):
            grad = dot(coef[base + k], qp_ref[:, halves[h]], TN)
            own_grad[h, k] = grad.reshape(net.depth, part, half)

    def query_side():
        for h in range(2):
            def add(b, acc):
                return acc + dot(coef[b], tab_block(h, b))

            acc = each_block(add, jnp.zeros((batch, half), F32))
            gq_ref[:, halves[h]] = acc.astype(BF16)
        d_queries[...] = dot(gq_ref[...], head[...], NT)
        for h in range(2):
            part_sum = dot(queries[...], gq_ref[:, halves[h]], TN)
            head_grad[h] = part_sum.reshape(head_grad.shape[1:])

    def rows_own(h, *at):
        return own_grad[(h,) + at]

    kept = net.scatter(sib, rows_own, out_grad, r0, r1, r2, stage, r3, query_side)
    row_grad = [k.astype(BF16) for k in kept]
    d_table[...] = dot(row_grad[0], head[:, halves[0]], NT) + dot(
        row_grad[1], head[:, halves[1]], NT
    )
    for h in range(2):
        part_sum = dot(my_table, row_grad[h], TN)
        head_grad[h] = head_grad[h] + part_sum.reshape(head_grad.shape[1:])
    if reduce_head:
        h_all, h_out, h0, h1, h2, h_stage, h3 = head_bufs
        sib, give = net.start_scatter(h_out, h0)
        for d in range(1, narrow):
            theirs = lax.rem(net.n + d, narrow) * 4
            for h in range(2):
                h_out[h, pl.ds(theirs, 4)] = head_grad[h, pl.ds(theirs, 4)].astype(BF16)
            give(d)

        def head_own(h, block, *at):
            return head_grad[(h, base + block) + at]

        kept = net.scatter(sib, head_own, h_out, h0, h1, h2, h_stage, h3)
        for h in range(2):
            h_all[h, base + me, z] = kept[h].astype(BF16)
        net.gather(h_all)
        for h in range(2):
            d_head[:, halves[h]] = h_all[h].astype(F32).reshape(width, half)
    else:
        for h in range(2):
            d_head[:, halves[h]] = head_grad[h].reshape(width, half)
    net.drain()


def per_device(queries, table, head, pos_ids, neg_ids, loss_weights):
    wide = lax.axis_size("wide")
    narrow = lax.axis_size("narrow")
    batch, width = queries.shape
    half = width // 2
    shard = table.shape[0]
    part = shard // narrow
    depth = wide // 4
    rows = shard * wide
    span = depth * part
    blocks = 4 * narrow
    reduce_head = width % (8 * wide * narrow) == 0
    ids = jnp.concatenate([neg_ids, pos_ids[:, None]], axis=1)
    owner, local = ids // shard, ids % shard
    ids = (local // part) * (wide * part) + (owner % 4) * span + (owner // 4) * part + local % part

    def scatter_bufs(height):
        return [
            pltpu.VMEM((2, blocks, depth, height, half), BF16),
            pltpu.VMEM((narrow - 1, 2, 4, depth, height, half), BF16),
            pltpu.VMEM((2, 2, depth, height, half), BF16),
            pltpu.VMEM((2, depth, height, half), BF16),
            pltpu.VMEM((4, depth, height, half), BF16),
            pltpu.VMEM((depth - 1, 2, height, half), BF16),
        ]

    scratch = [
        pltpu.VMEM((2, blocks, depth, part, half), BF16),
        pltpu.VMEM((batch, rows), F32),
        pltpu.VMEM((narrow, 1, rows), F32),
        pltpu.VMEM((batch, rows), F32),
        pltpu.VMEM((blocks, batch, span), BF16),
        pltpu.VMEM((batch, width), BF16),
        pltpu.VMEM((batch, width), BF16),
        pltpu.VMEM((2, 4, depth, part, half), F32),
    ] + scatter_bufs(part)
    if reduce_head:
        height = width // (wide * narrow)
        scratch.append(pltpu.VMEM((2, blocks, depth, height, half), F32))
        scratch.append(pltpu.VMEM((2, blocks, depth, height, half), BF16))
        scratch += scatter_bufs(height)
    else:
        scratch.append(pltpu.VMEM((2, width, half), F32))
    count = 2 * (6 * depth + 6 + 5 * narrow) + narrow
    sems = [pltpu.SemaphoreType.DMA((count,)), pltpu.SemaphoreType.DMA((count,))]
    vmem = pl.BlockSpec(memory_space=pltpu.VMEM)
    d_queries, d_table, d_head = pl.pallas_call(
        functools.partial(kernel, wide, narrow, reduce_head),
        out_shape=(
            jax.ShapeDtypeStruct((batch, width), F32),
            jax.ShapeDtypeStruct((part, width), F32),
            jax.ShapeDtypeStruct((width, width), F32),
        ),
        in_specs=[vmem] * 5,
        out_specs=(vmem,) * 3,
        scratch_shapes=sems + scratch,
        compiler_params=pltpu.CompilerParams(
            collective_id=0, has_side_effects=True, vmem_limit_bytes=60 * 1024 * 1024
        ),
    )(queries, table, head, ids, loss_weights[:, None])
    if not reduce_head:
        d_head = lax.psum(d_head, BOTH)
    return (d_queries, d_table, d_head)


def solution(mesh):
    placed = (
        P(BOTH, None),
        P("wide", None),
        P(),
        P(BOTH),
        P(BOTH, None),
        P(BOTH),
    )
    return jax.shard_map(
        per_device,
        mesh=mesh,
        in_specs=placed,
        out_specs=(P(BOTH, None), P(BOTH, None), P()),
        check_vma=False,
    )
```

time: 309 us -> 94.5 us (0.31)
  waiting for transfers between devices: 256 us -> 0 us
  Pallas kernels: 0 us -> 83.8 us
  matrix products: 20.9 us -> 0 us
  between operations: 14.1 us -> 0.64 us
  other arithmetic: 5.46 us -> 1.52 us
  starting transfers between devices: 3.6 us -> 0 us
    psum x1 -> x0, waiting for transfers between devices: 132 us -> none  [per_device(): d_head = lax.psum(head_part, BOTH)]
    pallas_call x0 -> x1, Pallas kernels: none -> 83.8 us  [per_device(): pl.pallas_call(functools.partial(kernel, wide, narrow, reduce_head), out_...]
    all_to_all x1 -> x0, waiting for transfers between devices: 66.1 us -> none  [per_device(): lax.all_to_all(row_partial, BOTH, split_axis=0, concat_axis=0, tiled=True)]
    all_gather x1 -> x0, waiting for transfers between devices: 57.6 us -> none  [per_device(): table_proj = lax.all_gather(my_proj, BOTH, axis=0, tiled=True)]
    dot_general x9 -> x0, matrix products: 20.9 us -> none  [the longest x1 4.24 us: per_device(): lax.dot_general(coef, query_proj, (((0,), (0,)), ((), ())), preferred_ele...]
    reduce_sum x3 -> x0, other arithmetic: 4.8 us -> none  [the longest x1 2.97 us: per_device(): jnp.sum(pieces.reshape(-1, part_rows, width).astype(jnp.float32), axis=0)]
    all_to_all x1 -> x0, starting transfers between devices: 3.52 us -> none  [per_device(): lax.all_to_all(row_partial, BOTH, split_axis=0, concat_axis=0, tiled=True)]
    unnamed x13 -> x3, local copies, waits for them, and re-layouts: 5.85 us -> 6.6 us
  transfers between devices with their start and end apart: 3 -> 0, of which waited for: 3 -> 0; matrix products, arithmetic and copies ran while one was open for 3% -> 0% of each run, Pallas kernels for 0% -> 0%
where the time goes in v2:
time: 94.5 us; the launch traced here: 94 us
  Pallas kernels  83.8 us (89%)
  local copies, waits for them, and re-layouts  8.11 us (9%)
  other arithmetic  1.52 us (2%)
    pallas_call x1, Pallas kernels, per_device(): pl.pallas_call(functools.partial(kernel, wide, narrow, reduce_head), out_...  83.8 us
    unnamed x3, local copies, waits for them, and re-layouts  6.6 us

profile of v2, /device:TPU:0, one launch (start us, length us, event | category | flops | bytes accessed | tf_op | source)
XLA Modules:
  0.0 94.0 jit_solution(4545881962106885032)
XLA Ops:
  0.6 0.7 pad_add_fusion
  1.3 0.1 copy.12
  1.5 0.8 fusion.3.ids
  2.3 1.4 %copy.16.weights = f32[128,1]{1,0:T(8,128)} copy(f32[128,1]{0,1:T(1,128)} %bitcast.2) | data formatting | bytes 1024 | tf_op jit(solution)/shard_map/broadcast_in_dim | solution.py:412
  3.7 83.8 %shard_map.85 = (f32[128,768]{1,0:T(8,128)}, f32[64,768]{1,0:T(8,128)}, f32[768,768]{1,0:T(8,128)}) custom-call(bf16[128,768]{1,0:T(8,128)(2,1)} %queries.1, bf16[128,768]{1,0:T(8,128)(2,1)} %table.1, bf16[768,768]{1,0:T(8,128)(2,1)} %head.1, s32[128,9]{1,0:T(8,128)} %fusion.3.ids, f32[128,1]{1,0:T(8,128)} %copy.16.weights), custom_call_target="tpu_custom_call" | custom-call | tf_op jit(solution)/shard_map/pallas_call | solution.py:399
  87.4 1.8 %copy.20 = f32[128,768]{1,0:T(8,128)} copy(f32[128,768]{1,0:T(8,128)} %get-tuple-element.6) | data formatting | bytes 786432
  89.2 1.6 %copy.21 = f32[64,768]{1,0:T(8,128)} copy(f32[64,768]{1,0:T(8,128)} %get-tuple-element.7) | data formatting | bytes 393216
  90.8 3.2 %copy.22 = f32[768,768]{1,0:T(8,128)} copy(f32[768,768]{1,0:T(8,128)} %get-tuple-element.8) | data formatting | bytes 4718592
